TPU v7x, 256 devices: a whole 4x4x8 slice. The times are simulated.
256 devices in a mesh: frames: 32 (over y, z), codes: 8 (over x, core).
Axes of the slice: x: 4, y: 4, z: 8, core: 2. Of those that a mesh axis runs over, the one named last changes fastest.
Arguments:
- frames: bfloat16 [262144, 256], P(('frames', 'codes')), may hold values from -32 to 32
- codes: bfloat16 [65536, 256], P('codes'), may hold values from -2 to 2
- pattern: int32 [2048, 48], P('frames'), may hold values from 0 to 512, as said below
Outputs:
- row_potential: float32 [262144], P('frames')
- col_potential: float32 [65536], P('codes')
Inputs may be any that keep to these rules, and one draw needn't show every extreme that they name: `pattern`: each row lists distinct code blocks in increasing order, padded at its end with 512; it lists at least one block, and at most 6 of the 64 blocks k*64 to (k+1)*64 - 1 of any group k, exactly 6 in some row; every code block is listed by some row.
All inputs are finite; a program needn't handle non-finite values.
Results may differ from a plain program's by a relative error of at most 0.0046.
Values may be sent and summed in bfloat16 or wider, within the bound.
No kernel may reach another device: no remote copies, remote signals or barrier semaphores. Data moves between devices by JAX's collectives and lax.ppermute only.
A program may use at most 128 MiB of HBM per device.

v0:
```python
import math

import jax
import jax.numpy as jnp
from jax import lax
from jax.sharding import Mesh
from jax.sharding import PartitionSpec as P

BLK = 128
GB = 64
CAP = 6
ITERS = 3
CODES = ("codes_0", "codes_1")
FRAMES = ("frames_0", "frames_1")
FRAMES_CODES = ("frames_0", "frames_1", "codes_0", "codes_1")


NEG_FILL = -1e30
LOGIT_SCALE = 2.0


def all_in_one(value, axis):
    leaves = jax.tree.leaves(value)
    turns = sorted(range(len(leaves)), key=lambda k: -leaves[k].size)
    width = (1, *leaves[turns[0]].shape)[-1]
    lines = [
        jnp.pad(leaves[k].reshape(-1), (0, -leaves[k].size % width)).reshape(-1, width)
        for k in turns
    ]
    both, at, found = (lax.all_gather(jnp.concatenate(lines), axis), 0, {})
    for k, line in zip(turns, lines):
        section = both[:, at : at + len(line)].reshape(len(both), -1)
        found[k] = section[:, : leaves[k].size].reshape(-1, *leaves[k].shape)
        at += len(line)
    numbers = iter(range(len(leaves)))
    return jax.tree.map(lambda _: found[next(numbers)], value)


def gathered_by_type(value, axis):
    leaves, found = (jax.tree.leaves(value), {})
    for leading, a in enumerate(leaves):
        if leading not in found:
            alike = [k for k, b in enumerate(leaves) if b.dtype == a.dtype]
            got = (
                all_in_one([leaves[k] for k in alike], axis)
                if len(alike) > 1
                else [lax.all_gather(a, axis)]
            )
            for k, b in zip(alike, got):
                found[k] = b
    numbers = iter(range(len(leaves)))
    return jax.tree.map(lambda _: found[next(numbers)], value)


def joined_all(value, axes, combine):
    for axis in axes:
        pieces = gathered_by_type(value, axis)
        value = jax.tree.map(lambda part: part[0], pieces)
        for k in range(1, lax.axis_size(axis)):
            value = combine(value, jax.tree.map(lambda part: part[k], pieces))
    return value


def combine_lse(earlier, later):
    highest = jnp.maximum(earlier[0], later[0])
    summed = earlier[1] * jnp.exp(earlier[0] - highest) + later[1] * jnp.exp(later[0] - highest)
    return (highest, summed)


def shards(frames, codes, pattern):
    gathered = lax.all_gather(frames, CODES, axis=0, tiled=True)
    feature_width = codes.shape[1]
    num_blocks = codes.shape[0] // BLK
    cap_here = CAP * (num_blocks // GB)
    frame_count = pattern.shape[0]
    slot_count = pattern.shape[1]
    low_block = lax.axis_index(CODES) * num_blocks
    first_pos = jnp.sum((pattern < low_block).astype(jnp.int32), axis=1)
    position = first_pos[:, None] + jnp.arange(cap_here, dtype=jnp.int32)[None, :]
    picked = jnp.take_along_axis(pattern, jnp.minimum(position, slot_count - 1), axis=1)
    usable = (position < slot_count) & (picked < low_block + num_blocks)
    local_block = jnp.clip(picked - low_block, 0, num_blocks - 1)
    code_blocks = codes.reshape(num_blocks, BLK, feature_width)[local_block]
    frame_blocks = gathered.reshape(frame_count, BLK, feature_width)
    product = jnp.einsum(
        "biw,bsjw->bsij", frame_blocks, code_blocks, preferred_element_type=jnp.float32
    )
    logits = (product * LOGIT_SCALE).astype(jnp.bfloat16)
    selector = (
        (local_block[:, :, None] == jnp.arange(num_blocks, dtype=jnp.int32)[None, None, :])
        & usable[:, :, None]
    ).reshape(frame_count * cap_here, num_blocks)
    selector_float = selector.astype(jnp.float32)
    tile_mask = usable[:, :, None, None]
    frames_total = frame_count * BLK * lax.axis_size(FRAMES)
    codes_total = num_blocks * BLK * lax.axis_size(CODES)
    log_ratio = math.log(frames_total / codes_total)
    col_potential = jnp.zeros((num_blocks, BLK), jnp.float32)
    row_potential = jnp.zeros((frame_count, BLK), jnp.float32)
    for iteration in range(ITERS):
        col_shift = jnp.dot(selector_float, col_potential, precision=lax.Precision.HIGHEST).reshape(
            frame_count, cap_here, BLK
        )
        scores = jnp.where(
            tile_mask, logits.astype(jnp.float32) + col_shift[:, :, None, :], NEG_FILL
        )
        local_high = jnp.max(scores, axis=(1, 3))
        local_sum = jnp.sum(
            jnp.where(tile_mask, jnp.exp(scores - local_high[:, None, :, None]), 0.0), axis=(1, 3)
        )
        row_high, row_sum = joined_all((local_high, local_sum), CODES, combine_lse)
        row_potential = -(row_high + jnp.log(row_sum))
        scores = jnp.where(
            tile_mask, logits.astype(jnp.float32) + row_potential[:, None, :, None], NEG_FILL
        )
        tile_high = jnp.max(scores, axis=2).reshape(frame_count * cap_here, BLK)
        local_col_high = jnp.max(
            jnp.where(selector[:, :, None], tile_high[:, None, :], NEG_FILL), axis=0
        )
        tile_ref = jnp.dot(selector_float, local_col_high, precision=lax.Precision.HIGHEST).reshape(
            frame_count, cap_here, BLK
        )
        tile_sum = jnp.sum(
            jnp.where(tile_mask, jnp.exp(scores - tile_ref[:, :, None, :]), 0.0), axis=2
        )
        local_col_sum = jnp.dot(
            selector_float.T,
            tile_sum.reshape(frame_count * cap_here, BLK),
            precision=lax.Precision.HIGHEST,
        )
        col_high, col_sum = joined_all((local_col_high, local_col_sum), FRAMES, combine_lse)
        col_potential = log_ratio - (col_high + jnp.log(col_sum))
    return (row_potential.reshape(-1), col_potential.reshape(-1))


def solution(mesh):
    torus = Mesh(mesh.devices.reshape(4, 8, 4, 2), ("frames_0", "frames_1", "codes_0", "codes_1"))
    placed = (P(FRAMES_CODES, None), P(CODES, None), P(FRAMES, None))
    return jax.shard_map(
        shards, mesh=torus, in_specs=placed, out_specs=(P(FRAMES), P(CODES)), check_vma=False
    )
```

profile of v0, /device:TPU:34, one launch (start us, length us, event | category | flops | bytes accessed | tf_op | source)
XLA Modules:
  0.0 374.6 jit_solution(14227339216331272537)
XLA Ops:
  7.9 0.8 convert_reduce_fusion
  8.9 4.4 %gather_fusion.1 = s32[384]{0:T(512)S(1)} fusion(s32[64,48]{0,1:T(8,128)} %param.5, s32[384]{0:T(512)S(1)} %reshape.570), kind=kCustom, calls=%fused_computation.1 | custom fusion | bytes 6144 | tf_op jit(solution)/shard_map/jit(take_along_axis)/gather | solution.py:80
  15.0 14.9 %gather_fusion = bf16[384,128,256]{2,1,0:T(8,128)(2,1)} fusion(bf16[64,128,256]{2,1,0:T(8,128)(2,1)} %bitcast.782, s32[1024]{0:T(1024)S(1)} %pad_clamp_fusion), kind=kCustom, calls=%fused_computation | custom fusion | bytes 50333184 | tf_op jit(solution)/shard_map/gather | solution.py:83
  30.2 15.8 %all-gather.14.cloned.1.call-done = bf16[8192,256]{1,0:T(8,128)(2,1)} async-done(((bf16[1024,256]{1,0:T(8,128)(2,1)}), bf16[8192,256]{1,0:T(8,128)(2,1)}) %all-gather.14.cloned.1.call-update) | async-done | bytes 4194320 | tf_op jit(solution)/shard_map/all_gather | solution.py:71
  46.0 13.5 %fusion.3 = (f32[64,128]{1,0:T(8,128)S(1)}, bf16[64,6,128,128]{3,2,1,0:T(8,128)(2,1)S(1)}) fusion(f32[64,6,128]{2,1,0:T(8,128)S(1)} %copy.84, pred[64,6]{1,0:T(8,128)(4,1)S(1)} %copy.107, bf16[64,6,128,256]{3,2,1,0:T(8,128)(2,1)} %bitcast.783, bf16[64,128,256,1]{2,1,3,0:T(8,128)(2,1)} %bitcast.797), kind=kOutput, calls=%fused_computation.11 | convolution fusion | flops 3258966016 | bytes 42172800 | tf_op jit(solution)/shard_map/biw,bsjw->bsij/dot_general | solution.py:85
  59.6 11.6 %fusion.6 = f32[64,128]{1,0:T(8,128)S(1)} fusion(bf16[64,6,128,128]{3,2,1,0:T(8,128)(2,1)S(1)} %get-tuple-element.19, f32[64,128]{1,0:T(8,128)S(1)} %get-tuple-element.18, f32[64,6,128]{2,1,0:T(8,128)S(1)} %copy.84, pred[64,6]{1,0:T(8,128)(4,1)S(1)} %copy.107), kind=kLoop, calls=%fused_computation.14 | loop fusion | flops 37740544 | bytes 12845440 | tf_op jit(solution)/shard_map/reduce_sum | solution.py:108
  71.2 11.4 %all-gather = f32[512,128]{1,0:T(8,128)S(1)} all-gather(f32[128,128]{1,0:T(8,128)S(1)} %pad_maximum_fusion), channel_id=2, replica_groups=mesh['frames_0'=4,'frames_1'=8,'codes_0'=4,'codes_1'=2] {'codes_0'}, dimensions={0}, use_global_device_ids=true | all-gather | bytes 327680 | tf_op jit(solution)/shard_map/all_gather | solution.py:30
  82.7 1.9 all-gather.1
  84.6 7.6 %fusion.10 = f32[64,6,128]{2,1,0:T(8,128)S(1)} fusion(bf16[64,6,128,128]{3,2,1,0:T(8,128)(2,1)S(1)} %get-tuple-element.19, f32[64,128]{1,0:T(8,128)S(1)} %fusion.209, pred[64,6]{1,0:T(8,128)(4,1)S(1)} %copy.107), kind=kLoop, calls=%fused_computation.18 | loop fusion | flops 25116672 | bytes 12812672 | tf_op jit(solution)/shard_map/reduce_max | solution.py:116
  92.3 4.5 %select_reduce_fusion.2 = f32[64,128]{1,0:T(8,128)S(1)} fusion(f32[384,128]{1,0:T(8,128)S(1)} %broadcast_in_dim.131, pred[384,64]{1,0:T(8,128)(4,1)S(1)} %fusion.51), kind=kLoop, calls=%fused_computation.53 | loop fusion | flops 6283264 | bytes 253952 | tf_op jit(solution)/shard_map/reduce_max | solution.py:117
  97.2 18.7 %fusion.13 = f32[64,6,128]{2,1,0:T(8,128)S(1)} fusion(bf16[64,6,128,128]{3,2,1,0:T(8,128)(2,1)} %copy-done, f32[64,6,128]{2,1,0:T(8,128)S(1)} %copy.88, f32[64,128]{1,0:T(8,128)S(1)} %fusion.209, pred[64,6]{1,0:T(8,128)(4,1)S(1)} %copy.107), kind=kLoop, calls=%fused_computation.21 | loop fusion | flops 37699584 | bytes 13009280 | tf_op jit(solution)/shard_map/reduce_sum | solution.py:123
  116.2 12.6 %all-gather.2 = f32[512,128]{1,0:T(8,128)S(1)} all-gather(f32[128,128]{1,0:T(8,128)S(1)} %pad_maximum_fusion.2), channel_id=4, replica_groups=mesh['frames_0'=4,'frames_1'=8,'codes_0'=4,'codes_1'=2] {'frames_0'}, dimensions={0}, use_global_device_ids=true | all-gather | bytes 327680 | tf_op jit(solution)/shard_map/all_gather | solution.py:30
  128.9 26.0 %all-gather.3 = f32[1024,128]{1,0:T(8,128)S(1)} all-gather(f32[128,128]{1,0:T(8,128)S(1)} %pad_maximum_fusion.3), channel_id=5, replica_groups=mesh['frames_0'=4,'frames_1'=8,'codes_0'=4,'codes_1'=2] {'frames_1'}, dimensions={0}, use_global_device_ids=true | all-gather | bytes 589824 | tf_op jit(solution)/shard_map/all_gather | solution.py:30
  155.3 8.3 %fusion.17 = f32[64,128]{1,0:T(8,128)S(1)} fusion(bf16[64,6,128,128]{3,2,1,0:T(8,128)(2,1)S(1)} %copy-done.1, f32[64,6,128]{2,1,0:T(8,128)S(1)} %copy.90, pred[64,6]{1,0:T(8,128)(4,1)S(1)} %copy.107), kind=kLoop, calls=%fused_computation.25 | loop fusion | flops 25157632 | bytes 12812672 | tf_op jit(solution)/shard_map/reduce_max | solution.py:107
  163.7 11.7 %fusion.20 = f32[64,128]{1,0:T(8,128)S(1)} fusion(bf16[64,6,128,128]{3,2,1,0:T(8,128)(2,1)S(1)} %copy-done.1, f32[64,128]{1,0:T(8,128)S(1)} %fusion.17, f32[64,6,128]{2,1,0:T(8,128)S(1)} %copy.90, pred[64,6]{1,0:T(8,128)(4,1)S(1)} %copy.107), kind=kLoop, calls=%fused_computation.28 | loop fusion | flops 37740544 | bytes 12845440 | tf_op jit(solution)/shard_map/reduce_sum | solution.py:108
  175.4 12.3 %all-gather.4 = f32[512,128]{1,0:T(8,128)S(1)} all-gather(f32[128,128]{1,0:T(8,128)S(1)} %pad_maximum_fusion.4), channel_id=6, replica_groups=mesh['frames_0'=4,'frames_1'=8,'codes_0'=4,'codes_1'=2] {'codes_0'}, dimensions={0}, use_global_device_ids=true | all-gather | bytes 327680 | tf_op jit(solution)/shard_map/all_gather | solution.py:30
  187.7 2.1 all-gather.5
  189.8 7.6 %fusion.24 = f32[64,6,128]{2,1,0:T(8,128)S(1)} fusion(bf16[64,6,128,128]{3,2,1,0:T(8,128)(2,1)S(1)} %copy-done.1, f32[64,128]{1,0:T(8,128)S(1)} %fusion.161, pred[64,6]{1,0:T(8,128)(4,1)S(1)} %copy.107), kind=kLoop, calls=%fused_computation.32 | loop fusion | flops 25116672 | bytes 12812672 | tf_op jit(solution)/shard_map/reduce_max | solution.py:116
  197.5 4.5 %select_reduce_fusion.1 = f32[64,128]{1,0:T(8,128)S(1)} fusion(f32[384,128]{1,0:T(8,128)S(1)} %broadcast_in_dim.134, pred[384,64]{1,0:T(8,128)(4,1)S(1)} %fusion.51), kind=kLoop, calls=%fused_computation.52 | loop fusion | flops 6283264 | bytes 253952 | tf_op jit(solution)/shard_map/reduce_max | solution.py:117
  202.5 18.7 %fusion.27 = f32[64,6,128]{2,1,0:T(8,128)S(1)} fusion(bf16[64,6,128,128]{3,2,1,0:T(8,128)(2,1)} %copy-done, f32[64,6,128]{2,1,0:T(8,128)S(1)} %copy.94, f32[64,128]{1,0:T(8,128)S(1)} %fusion.161, pred[64,6]{1,0:T(8,128)(4,1)S(1)} %copy.107), kind=kLoop, calls=%fused_computation.35 | loop fusion | flops 37699584 | bytes 13009280 | tf_op jit(solution)/shard_map/reduce_sum | solution.py:123
  221.5 12.4 %all-gather.6 = f32[512,128]{1,0:T(8,128)S(1)} all-gather(f32[128,128]{1,0:T(8,128)S(1)} %pad_maximum_fusion.6), channel_id=8, replica_groups=mesh['frames_0'=4,'frames_1'=8,'codes_0'=4,'codes_1'=2] {'frames_0'}, dimensions={0}, use_global_device_ids=true | all-gather | bytes 327680 | tf_op jit(solution)/shard_map/all_gather | solution.py:30
  233.9 25.4 %all-gather.7 = f32[1024,128]{1,0:T(8,128)S(1)} all-gather(f32[128,128]{1,0:T(8,128)S(1)} %pad_maximum_fusion.7), channel_id=9, replica_groups=mesh['frames_0'=4,'frames_1'=8,'codes_0'=4,'codes_1'=2] {'frames_1'}, dimensions={0}, use_global_device_ids=true | all-gather | bytes 589824 | tf_op jit(solution)/shard_map/all_gather | solution.py:30
  259.8 9.8 %fusion.31 = f32[64,128]{1,0:T(8,128)S(1)} fusion(bf16[64,6,128,128]{3,2,1,0:T(8,128)(2,1)} %copy-done, f32[64,6,128]{2,1,0:T(8,128)S(1)} %copy.96, pred[64,6]{1,0:T(8,128)(4,1)S(1)} %copy.107), kind=kLoop, calls=%fused_computation.39 | loop fusion | flops 25157632 | bytes 12812672 | tf_op jit(solution)/shard_map/reduce_max | solution.py:107
  269.6 13.1 %fusion.34 = f32[64,128]{1,0:T(8,128)S(1)} fusion(bf16[64,6,128,128]{3,2,1,0:T(8,128)(2,1)} %copy-done, f32[64,128]{1,0:T(8,128)S(1)} %fusion.31, f32[64,6,128]{2,1,0:T(8,128)S(1)} %copy.96, pred[64,6]{1,0:T(8,128)(4,1)S(1)} %copy.107), kind=kLoop, calls=%fused_computation.42 | loop fusion | flops 37740544 | bytes 12845440 | tf_op jit(solution)/shard_map/reduce_sum | solution.py:108
  282.7 12.3 %all-gather.8 = f32[512,128]{1,0:T(8,128)S(1)} all-gather(f32[128,128]{1,0:T(8,128)S(1)} %pad_maximum_fusion.8), channel_id=10, replica_groups=mesh['frames_0'=4,'frames_1'=8,'codes_0'=4,'codes_1'=2] {'codes_0'}, dimensions={0}, use_global_device_ids=true | all-gather | bytes 327680 | tf_op jit(solution)/shard_map/all_gather | solution.py:30
  295.0 1.9 all-gather.9
  297.6 7.6 %fusion.38 = f32[64,6,128]{2,1,0:T(8,128)S(1)} fusion(bf16[64,6,128,128]{3,2,1,0:T(8,128)(2,1)S(1)} %bitcast.781, f32[64,128]{1,0:T(8,128)S(1)} %fusion.224, pred[64,6]{1,0:T(8,128)(4,1)S(1)} %copy.107), kind=kLoop, calls=%fused_computation.46 | loop fusion | flops 25116672 | bytes 12812672 | tf_op jit(solution)/shard_map/reduce_max | solution.py:116
  305.3 4.5 %select_reduce_fusion = f32[64,128]{1,0:T(8,128)S(1)} fusion(f32[384,128]{1,0:T(8,128)S(1)} %broadcast_in_dim.136, pred[384,64]{1,0:T(8,128)(4,1)S(1)} %fusion.51), kind=kLoop, calls=%fused_computation.51 | loop fusion | flops 6283264 | bytes 253952 | tf_op jit(solution)/shard_map/reduce_max | solution.py:117
  310.2 18.7 %fusion.41 = f32[64,6,128]{2,1,0:T(8,128)S(1)} fusion(bf16[64,6,128,128]{3,2,1,0:T(8,128)(2,1)} %copy-done, f32[64,6,128]{2,1,0:T(8,128)S(1)} %copy.100, f32[64,128]{1,0:T(8,128)S(1)} %fusion.224, pred[64,6]{1,0:T(8,128)(4,1)S(1)} %copy.107), kind=kLoop, calls=%fused_computation.49 | loop fusion | flops 37699584 | bytes 13009280 | tf_op jit(solution)/shard_map/reduce_sum | solution.py:123
  329.2 12.3 %all-gather.10 = f32[512,128]{1,0:T(8,128)S(1)} all-gather(f32[128,128]{1,0:T(8,128)S(1)} %pad_maximum_fusion.10), channel_id=12, replica_groups=mesh['frames_0'=4,'frames_1'=8,'codes_0'=4,'codes_1'=2] {'frames_0'}, dimensions={0}, use_global_device_ids=true | all-gather | bytes 327680 | tf_op jit(solution)/shard_map/all_gather | solution.py:30
  341.6 25.4 %all-gather.11 = f32[1024,128]{1,0:T(8,128)S(1)} all-gather(f32[128,128]{1,0:T(8,128)S(1)} %pad_maximum_fusion.11), channel_id=13, replica_groups=mesh['frames_0'=4,'frames_1'=8,'codes_0'=4,'codes_1'=2] {'frames_1'}, dimensions={0}, use_global_device_ids=true | all-gather | bytes 589824 | tf_op jit(solution)/shard_map/all_gather | solution.py:30
  367.0 0.7 fusion.86
  (71 shorter events, 7.1 us)
Async XLA Ops:
  7.2 38.9 %all-gather.14.cloned.1.call-start = ((), (), s32[]{:S(2)}) async-start(), calls=%async_computation | async-start | bytes 4718592 | tf_op jit(solution)/shard_map/all_gather | solution.py:71
  59.6 25.1 %copy-start = (bf16[64,6,128,128]{3,2,1,0:T(8,128)(2,1)}, bf16[64,6,128,128]{3,2,1,0:T(8,128)(2,1)S(1)}, u32[]{:S(2)}) copy-start(bf16[64,6,128,128]{3,2,1,0:T(8,128)(2,1)S(1)} %get-tuple-element.19) | copy-start | bytes 37748740
  92.2 63.1 %copy-start.1 = (bf16[64,6,128,128]{3,2,1,0:T(8,128)(2,1)S(1)}, bf16[64,6,128,128]{3,2,1,0:T(8,128)(2,1)}, u32[]{:S(2)}) copy-start(bf16[64,6,128,128]{3,2,1,0:T(8,128)(2,1)} %copy-done) | copy-start | bytes 37748740
  197.5 100.1 %slice-start = ((s8[12582912]{0:T(1024)(128)(4,1)}), s8[4194304]{0:T(1024)(128)(4,1)S(1)}, s32[]{:S(2)}) async-start(s8[12582912]{0:T(1024)(128)(4,1)} %bitcast.780), calls=%async_computation.1 | async-start | bytes 8388608
  221.5 76.2 %slice-start.1 = ((s8[12582912]{0:T(1024)(128)(4,1)}), s8[4194304]{0:T(1024)(128)(4,1)S(1)}, s32[]{:S(2)}) async-start(s8[12582912]{0:T(1024)(128)(4,1)} %bitcast.780), calls=%async_computation.2 | async-start | bytes 8388608
  259.8 37.8 %slice-start.2 = ((s8[12582912]{0:T(1024)(128)(4,1)}), s8[4194304]{0:T(1024)(128)(4,1)S(1)}, s32[]{:S(2)}) async-start(s8[12582912]{0:T(1024)(128)(4,1)} %bitcast.780), calls=%async_computation.3 | async-start | bytes 8388608
Sparse Core Ops, SparseCore 0:
  9.8 36.1 all-gather.13
where the time goes:
time: 379 us; the launch traced here: 375 us
  blocking collectives  156 us (41%)
  other arithmetic  150 us (40%)
  local copies, waits for them, and re-layouts  21.4 us (6%)
  waiting for transfers between devices  16.5 us (4%)
  matrix products  16.4 us (4%)
  between operations  14.5 us (4%)
    all_gather x12, blocking collectives, all_in_one(): both, at, found = (lax.all_gather(jnp.concatenate(lines), axis), 0, {})  156 us
    reduce_sum x3, other arithmetic, shards(): jnp.sum(jnp.where(tile_mask, jnp.exp(scores - tile_ref[:, :, None, :]), 0...  56.1 us
    reduce_sum x3, other arithmetic, shards(): jnp.sum(jnp.where(tile_mask, jnp.exp(scores - local_high[:, None, :, None...  36.4 us
    reduce_max x3, other arithmetic, shards(): tile_high = jnp.max(scores, axis=2).reshape(frame_count * cap_here, BLK)  22.8 us
    reduce_max x2, other arithmetic, shards(): local_high = jnp.max(scores, axis=(1, 3))  18.1 us
    all_gather x1, waiting for transfers between devices, shards(): gathered = lax.all_gather(frames, CODES, axis=0, tiled=True)  15.8 us
    gather x1, local copies, waits for them, and re-layouts, shards(): code_blocks = codes.reshape(num_blocks, BLK, feature_width)[local_block]  14.9 us
    dot_general x1, matrix products, shards(): jnp.einsum('biw,bsjw->bsij', frame_blocks, code_blocks, preferred_element...  13.5 us
  transfers between devices with their start and end apart: 1, of which 1 were waited for; matrix products, arithmetic and copies ran while one was open for 6% of the time, Pallas kernels for 0%

commit v1 on v0

v1 whole, which is shorter than its diff:
```python
import functools
import math

import jax
import jax.numpy as jnp
from jax import lax
from jax.experimental import pallas as pl
from jax.experimental.pallas import tpu as pltpu
from jax.sharding import Mesh
from jax.sharding import PartitionSpec as P

BLK = 128
GB = 64
CAP = 6
ITERS = 3
PER = 8
CODES = ("codes_0", "codes_1")
FRAMES = ("frames_0", "frames_1")
FRAMES_CODES = ("frames_0", "frames_1", "codes_0", "codes_1")

NEG_FILL = -1e30
NEG_ROW = -1e29
SMALL = 1e-26
VMEM = 56 * 1024 * 1024


def tiles_kernel(picks, frames_ref, codes_ref, exp_ref, logit_ref, high_ref, lse_ref):
    group = pl.program_id(0)
    for b in range(PER):
        lanes = slice(b * BLK, (b + 1) * BLK)
        block = frames_ref[lanes, :] * jnp.bfloat16(2.0)
        top = None
        for s in range(CAP):
            pick = picks[(group * PER + b) * 8 + s]
            chosen = codes_ref[jnp.maximum(pick, 0)]
            tile = lax.dot_general(
                chosen, block, (((1,), (1,)), ((), ())), preferred_element_type=jnp.float32
            )
            tile = jnp.where(pick >= 0, tile, NEG_FILL).astype(jnp.bfloat16)
            logit_ref[0, s * BLK : (s + 1) * BLK, lanes] = tile
            part = jnp.max(tile.astype(jnp.float32).reshape(BLK // 8, 8, BLK), axis=0)
            top = part if top is None else jnp.maximum(top, part)
        high = jnp.maximum(jnp.max(top, axis=0, keepdims=True), NEG_ROW)
        total = None
        for s in range(CAP):
            tile = logit_ref[0, s * BLK : (s + 1) * BLK, lanes].astype(jnp.float32)
            terms = jnp.exp(tile - high)
            exp_ref[0, s * BLK : (s + 1) * BLK, lanes] = terms.astype(jnp.bfloat16)
            part = jnp.sum(terms.reshape(BLK // 8, 8, BLK), axis=0)
            total = part if total is None else total + part
        total = jnp.sum(total, axis=0, keepdims=True)
        high_ref[b : b + 1, :] = high
        lse_ref[b : b + 1, :] = jnp.where(total > 0.0, high + jnp.log(total), NEG_FILL)


def make_tiles(picks, frames, codes):
    groups = frames.shape[0] // (PER * BLK)
    rows = groups * PER
    return pl.pallas_call(
        tiles_kernel,
        grid_spec=pltpu.PrefetchScalarGridSpec(
            num_scalar_prefetch=1,
            grid=(groups,),
            in_specs=[
                pl.BlockSpec((PER * BLK, frames.shape[1]), lambda g, _: (g, 0)),
                pl.BlockSpec(codes.shape, lambda g, _: (0, 0, 0), pipeline_mode=pl.Buffered(1)),
            ],
            out_specs=[
                pl.BlockSpec((1, CAP * BLK, PER * BLK), lambda g, _: (g, 0, 0)),
                pl.BlockSpec((1, CAP * BLK, PER * BLK), lambda g, _: (g, 0, 0)),
                pl.BlockSpec((PER, BLK), lambda g, _: (g, 0)),
                pl.BlockSpec((PER, BLK), lambda g, _: (g, 0)),
            ],
        ),
        out_shape=[
            jax.ShapeDtypeStruct((groups, CAP * BLK, PER * BLK), jnp.bfloat16),
            jax.ShapeDtypeStruct((groups, CAP * BLK, PER * BLK), jnp.bfloat16),
            jax.ShapeDtypeStruct((rows, BLK), jnp.float32),
            jax.ShapeDtypeStruct((rows, BLK), jnp.float32),
        ],
        compiler_params=pltpu.CompilerParams(vmem_limit_bytes=VMEM),
        name="make_tiles",
    )(picks, frames, codes)


def log_sum(pieces_ref):
    count = pieces_ref.shape[0]
    high = pieces_ref[0]
    for k in range(1, count):
        high = jnp.maximum(high, pieces_ref[k])
    total = jnp.exp(pieces_ref[0] - high)
    for k in range(1, count):
        total = total + jnp.exp(pieces_ref[k] - high)
    return high + jnp.log(total)


def split_dot(selector, values):
    upper = values.astype(jnp.bfloat16)
    lower = (values - upper.astype(jnp.float32)).astype(jnp.bfloat16)
    return jnp.dot(selector, upper, preferred_element_type=jnp.float32) + jnp.dot(
        selector, lower, preferred_element_type=jnp.float32
    )


def stable_pass(picks, logit_ref, shift_ref, out_ref, block_ref, high_ref, total_ref, by_code):
    high_ref[...] = jnp.full_like(high_ref, NEG_FILL)
    total_ref[...] = jnp.zeros_like(total_ref)

    def one_group(g, _):
        pltpu.sync_copy(logit_ref.at[g], block_ref)

        def one_tile(index, _):
            b = index // CAP
            s = index - b * CAP
            row = g * PER + b
            pick = picks[row * 8 + s]

            @pl.when(pick >= 0)
            def _():
                rows = pl.ds(pl.multiple_of(s * BLK, BLK), BLK)
                lanes = pl.ds(pl.multiple_of(b * BLK, BLK), BLK)
                tile = block_ref[rows, lanes].astype(jnp.float32)
                if by_code:
                    tile = jnp.transpose(tile + shift_ref[pl.ds(row, 1), :])
                    at = pl.ds(pick, 1)
                else:
                    shift = jnp.broadcast_to(shift_ref[pl.ds(pick, 1), :], (BLK, BLK))
                    tile = tile + jnp.transpose(shift)
                    at = pl.ds(row, 1)
                before = high_ref[at, :]
                high = jnp.maximum(before, jnp.max(tile, axis=0, keepdims=True))
                total_ref[at, :] = total_ref[at, :] * jnp.exp(before - high) + jnp.sum(
                    jnp.exp(tile - high), axis=0, keepdims=True
                )
                high_ref[at, :] = high

            return 0

        lax.fori_loop(0, CAP * PER, one_tile, 0)
        return 0

    lax.fori_loop(0, logit_ref.shape[0], one_group, 0)
    total = total_ref[...]
    out_ref[...] = jnp.where(
        total > 0.0, high_ref[...] + jnp.log(jnp.maximum(total, 1e-37)), NEG_FILL
    )


def column_kernel(
    copies, picks, pieces_ref, high_ref, picks_ref, exp_ref, logit_ref, row_ref, out_ref,
    scale_ref, sums_ref, peak_ref, lse_ref, block_ref, top_ref, total_ref,
):
    group = pl.program_id(0)

    @pl.when(group == 0)
    def _():
        row = -log_sum(pieces_ref)
        row_ref[...] = row
        weight = high_ref[...] + row
        peak = jnp.max(weight)
        peak_ref[0] = peak
        scale_ref[...] = jnp.exp(weight - peak)

    scale = scale_ref[pl.ds(pl.multiple_of(group * PER, PER), PER), :]
    wide = jnp.concatenate([scale] * PER, axis=1)
    lane_block = lax.broadcasted_iota(jnp.int32, wide.shape, 1) // BLK
    row_block = lax.broadcasted_iota(jnp.int32, wide.shape, 0)
    wide = jnp.where(lane_block == row_block, wide, 0.0).astype(jnp.bfloat16)
    sums_ref[pl.ds(pl.multiple_of(group * PER, PER), PER), :] = lax.dot_general(
        wide, exp_ref[0], (((1,), (1,)), ((), ())), preferred_element_type=jnp.float32
    )

    @pl.when(group == pl.num_programs(0) - 1)
    def _():
        blocks = lax.broadcasted_iota(jnp.int32, (GB, picks_ref.shape[1]), 0)
        total = jnp.zeros(lse_ref.shape, jnp.float32)
        used = jnp.zeros((GB, 1), jnp.float32)
        for s in range(CAP):
            hit = (picks_ref[s : s + 1, :] == blocks).astype(jnp.float32)
            used = used + jnp.sum(hit, axis=1, keepdims=True)
            total = total + split_dot(
                hit.astype(jnp.bfloat16), sums_ref[:, s * BLK : (s + 1) * BLK]
            )
        lse_ref[...] = jnp.where(
            total > 0.0, peak_ref[0] + jnp.log(jnp.maximum(total, 1e-37)), NEG_FILL
        )
        low = jnp.min(jnp.where(used > 0.0, total, 1.0))

        @pl.when(jnp.logical_not(low >= SMALL))
        def _():
            stable_pass(
                picks, logit_ref, row_ref, lse_ref, block_ref, top_ref, total_ref, True
            )

        for k in range(copies):
            out_ref[k] = lse_ref[...]


def row_kernel(
    copies, log_ratio, picks, pieces_ref, high_ref, picks_ref, exp_ref, logit_ref, out_ref,
    col_ref, scale_ref, sums_ref, peak_ref, lse_ref, block_ref, top_ref, total_ref,
):
    group = pl.program_id(0)

    @pl.when(group == 0)
    def _():
        col = log_ratio - log_sum(pieces_ref)
        col_ref[...] = col
        peak = jnp.max(col)
        peak_ref[0] = peak
        scale = jnp.exp(col - peak).astype(jnp.bfloat16)
        blocks = lax.broadcasted_iota(jnp.int32, (picks_ref.shape[0], GB), 1)
        for s in range(CAP):
            hit = (picks_ref[:, s : s + 1] == blocks).astype(jnp.float32).astype(jnp.bfloat16)
            scale_ref[:, s * BLK : (s + 1) * BLK] = jnp.dot(
                hit, scale, preferred_element_type=jnp.float32
            )

    at = pl.ds(pl.multiple_of(group * PER, PER), PER)
    scale = scale_ref[at, :].astype(jnp.bfloat16)
    wide = jnp.dot(scale, exp_ref[0], preferred_element_type=jnp.float32)
    row_block = lax.broadcasted_iota(jnp.int32, (PER, BLK), 0)
    total = jnp.zeros((PER, BLK), jnp.float32)
    for b in range(PER):
        total = total + jnp.where(row_block == b, wide[:, b * BLK : (b + 1) * BLK], 0.0)
    sums_ref[at, :] = total

    @pl.when(group == pl.num_programs(0) - 1)
    def _():
        total = sums_ref[...]
        lse_ref[...] = jnp.where(
            total > 0.0,
            high_ref[...] + (peak_ref[0] + jnp.log(jnp.maximum(total, 1e-37))),
            NEG_FILL,
        )
        low = jnp.min(jnp.where(picks_ref[:, 0:1] >= 0, total, 1.0))

        @pl.when(jnp.logical_not(low >= SMALL))
        def _():
            stable_pass(
                picks, logit_ref, col_ref, lse_ref, block_ref, top_ref, total_ref, False
            )

        for k in range(copies):
            out_ref[k] = lse_ref[...]


def whole(array):
    zeros = (0,) * array.ndim
    return pl.BlockSpec(array.shape, lambda g, _: zeros, pipeline_mode=pl.Buffered(1))


def column_pass(picks, pieces, high, picks_t, exps, logits, copies):
    groups = exps.shape[0]
    rows = high.shape[0]
    return pl.pallas_call(
        functools.partial(column_kernel, copies),
        grid_spec=pltpu.PrefetchScalarGridSpec(
            num_scalar_prefetch=1,
            grid=(groups,),
            in_specs=[
                whole(pieces),
                whole(high),
                whole(picks_t),
                pl.BlockSpec((1, *exps.shape[1:]), lambda g, _: (g, 0, 0)),
                pl.BlockSpec(memory_space=pl.ANY),
            ],
            out_specs=[
                pl.BlockSpec((rows, BLK), lambda g, _: (0, 0)),
                pl.BlockSpec((copies, GB, BLK), lambda g, _: (0, 0, 0)),
            ],
            scratch_shapes=[
                pltpu.VMEM((rows, BLK), jnp.float32),
                pltpu.VMEM((rows, CAP * BLK), jnp.float32),
                pltpu.SMEM((1,), jnp.float32),
                pltpu.VMEM((GB, BLK), jnp.float32),
                pltpu.VMEM(exps.shape[1:], jnp.bfloat16),
                pltpu.VMEM((GB, BLK), jnp.float32),
                pltpu.VMEM((GB, BLK), jnp.float32),
            ],
        ),
        out_shape=[
            jax.ShapeDtypeStruct((rows, BLK), jnp.float32),
            jax.ShapeDtypeStruct((copies, GB, BLK), jnp.float32),
        ],
        compiler_params=pltpu.CompilerParams(vmem_limit_bytes=VMEM),
        name="column_pass",
    )(picks, pieces, high, picks_t, exps, logits)


def row_pass(picks, pieces, high, picks_v, exps, logits, copies, log_ratio):
    groups = exps.shape[0]
    rows = high.shape[0]
    return pl.pallas_call(
        functools.partial(row_kernel, copies, log_ratio),
        grid_spec=pltpu.PrefetchScalarGridSpec(
            num_scalar_prefetch=1,
            grid=(groups,),
            in_specs=[
                whole(pieces),
                whole(high),
                whole(picks_v),
                pl.BlockSpec((1, *exps.shape[1:]), lambda g, _: (g, 0, 0)),
                pl.BlockSpec(memory_space=pl.ANY),
            ],
            out_specs=pl.BlockSpec((copies, rows, BLK), lambda g, _: (0, 0, 0)),
            scratch_shapes=[
                pltpu.VMEM((GB, BLK), jnp.float32),
                pltpu.VMEM((rows, CAP * BLK), jnp.float32),
                pltpu.VMEM((rows, BLK), jnp.float32),
                pltpu.SMEM((1,), jnp.float32),
                pltpu.VMEM((rows, BLK), jnp.float32),
                pltpu.VMEM(exps.shape[1:], jnp.bfloat16),
                pltpu.VMEM((rows, BLK), jnp.float32),
                pltpu.VMEM((rows, BLK), jnp.float32),
            ],
        ),
        out_shape=jax.ShapeDtypeStruct((copies, rows, BLK), jnp.float32),
        compiler_params=pltpu.CompilerParams(vmem_limit_bytes=VMEM),
        name="row_pass",
    )(picks, pieces, high, picks_v, exps, logits)


def candidates(pattern, low_block):
    rows, slots = pattern.shape
    first = jnp.sum((pattern < low_block).astype(jnp.int32), axis=1)
    position = first[:, None] + jnp.arange(8, dtype=jnp.int32)[None, :]
    here = position[:, :, None] == jnp.arange(slots, dtype=jnp.int32)[None, None, :]
    offset = pattern - low_block
    found = jnp.max(jnp.where(here, offset[:, None, :], -1), axis=2)
    fits = (found < GB) & (jnp.arange(8, dtype=jnp.int32)[None, :] < CAP)
    return jnp.where(fits, found, -1)


def shards(frames, codes, pattern):
    gathered = lax.all_gather(frames, CODES, axis=0, tiled=True)
    feature_width = codes.shape[1]
    num_blocks = codes.shape[0] // BLK
    frame_count = pattern.shape[0]
    picked = candidates(pattern, lax.axis_index(CODES) * num_blocks)
    picks = picked.reshape(-1)
    frames_total = frame_count * BLK * lax.axis_size(FRAMES)
    codes_total = num_blocks * BLK * lax.axis_size(CODES)
    log_ratio = math.log(frames_total / codes_total)
    code_copies = lax.axis_size(CODES)
    frame_copies = lax.axis_size(FRAMES)
    exps, logits, high, lse = make_tiles(
        picks, gathered, codes.reshape(num_blocks, BLK, feature_width)
    )
    pieces = jnp.broadcast_to(lse[None], (code_copies, *lse.shape))
    for iteration in range(ITERS):
        pieces = lax.all_to_all(pieces, CODES, 0, 0, tiled=True)
        row_potential, pieces = column_pass(
            picks, pieces, high, picked.T, exps, logits, frame_copies
        )
        pieces = lax.all_to_all(pieces, FRAMES, 0, 0, tiled=True)
        if iteration < ITERS - 1:
            pieces = row_pass(
                picks, pieces, high, picked, exps, logits, code_copies, log_ratio
            )
    highest = jnp.max(pieces, axis=0)
    summed = jnp.sum(jnp.exp(pieces - highest[None]), axis=0)
    col_potential = log_ratio - (highest + jnp.log(summed))
    return (row_potential.reshape(-1), col_potential.reshape(-1))


def solution(mesh):
    torus = Mesh(mesh.devices.reshape(4, 8, 4, 2), ("frames_0", "frames_1", "codes_0", "codes_1"))
    placed = (P(FRAMES_CODES, None), P(CODES, None), P(FRAMES, None))
    return jax.shard_map(
        shards, mesh=torus, in_specs=placed, out_specs=(P(FRAMES), P(CODES)), check_vma=False
    )
```

time: 379 us -> 507 us (1.34)
  blocking collectives: 156 us -> 319 us
  other arithmetic: 150 us -> 3.57 us
  Pallas kernels: 0 us -> 73.6 us
  waiting for transfers between devices: 16.5 us -> 69.9 us
  local copies, waits for them, and re-layouts: 21.4 us -> 3.63 us
  matrix products: 16.4 us -> 0 us
  starting transfers between devices: 0.04 us -> 15 us
    all_to_all x0 -> x4, blocking collectives: none -> 319 us  [the longest x2 200 us: shards(): pieces = lax.all_to_all(pieces, CODES, 0, 0, tiled=True)]
    all_gather x12 -> x0, blocking collectives: 156 us -> none  [all_in_one(): both, at, found = (lax.all_gather(jnp.concatenate(lines), axis), 0, {})]
    reduce_sum x7 -> x2, other arithmetic: 93.2 us -> 0.92 us  [the longest x1 0.76 us: candidates(): first = jnp.sum((pattern < low_block).astype(jnp.int32), axis=1)]
    pallas_call x0 -> x6, Pallas kernels: none -> 73.6 us  [the longest x3 33 us: column_pass(): pl.pallas_call(functools.partial(column_kernel, copies), grid_spec=pltpu....]
    reduce_max x8 -> x2, other arithmetic: 54.4 us -> 0.12 us  [the longest x1 0.07 us: shards(): highest = jnp.max(pieces, axis=0)]
    all_to_all x0 -> x2, waiting for transfers between devices: none -> 32.8 us  [the longest x1 27.4 us: shards(): pieces = lax.all_to_all(pieces, FRAMES, 0, 0, tiled=True)]
    all_gather x1, waiting for transfers between devices: 15.8 us -> 36.4 us  [shards(): gathered = lax.all_gather(frames, CODES, axis=0, tiled=True)]
    gather x6 -> x0, local copies, waits for them, and re-layouts: 19.8 us -> none  [the longest x1 14.9 us: shards(): code_blocks = codes.reshape(num_blocks, BLK, feature_width)[local_block]]
  transfers between devices with their start and end apart: 1 -> 3, of which waited for: 1 -> 3; matrix products, arithmetic and copies ran while one was open for 6% -> 1% of each run, Pallas kernels for 0% -> 0%
where the time goes in v1:
time: 507 us; the launch traced here: 498 us
  blocking collectives  319 us (63%)
  Pallas kernels  73.6 us (15%)
  waiting for transfers between devices  69.9 us (14%)
  starting transfers between devices  15 us (3%)
  between operations  14.1 us (3%)
    all_to_all x2, blocking collectives, shards(): pieces = lax.all_to_all(pieces, CODES, 0, 0, tiled=True)  200 us
    all_to_all x2, blocking collectives, shards(): pieces = lax.all_to_all(pieces, FRAMES, 0, 0, tiled=True)  118 us
    all_gather x1, waiting for transfers between devices, shards(): gathered = lax.all_gather(frames, CODES, axis=0, tiled=True)  36.4 us
    pallas_call x3, Pallas kernels, column_pass(): pl.pallas_call(functools.partial(column_kernel, copies), grid_spec=pltpu....  33 us
    all_to_all x1, waiting for transfers between devices, shards(): pieces = lax.all_to_all(pieces, FRAMES, 0, 0, tiled=True)  27.4 us
    pallas_call x1, Pallas kernels, make_tiles(): pl.pallas_call(tiles_kernel, grid_spec=pltpu.PrefetchScalarGridSpec(num_s...  20.5 us
    pallas_call x2, Pallas kernels, row_pass(): pl.pallas_call(functools.partial(row_kernel, copies, log_ratio), grid_spe...  20.2 us
  transfers between devices with their start and end apart: 3, of which 3 were waited for; matrix products, arithmetic and copies ran while one was open for 1% of the time, Pallas kernels for 0%

profile of v1, /device:TPU:34, one launch (start us, length us, event | category | flops | bytes accessed | tf_op | source)
XLA Modules:
  0.0 498.4 jit_solution(8971767267913440510)
XLA Ops:
  7.2 0.0 all-gather.2.cloned.1.call-start
  7.2 0.7 all-gather.2.cloned.1.call-update
  7.9 0.1 and.23
  8.0 0.8 convert_reduce_fusion
  8.8 0.1 select_reduce_fusion
  8.9 0.1 copy.17
  8.9 0.1 reduce_max.23
  9.0 0.6 and_select_fusion.1.picks
  9.6 36.4 %all-gather.2.cloned.1.call-done.frames_ref = bf16[8192,256]{1,0:T(8,128)(2,1)} async-done(((bf16[1024,256]{1,0:T(8,128)(2,1)}), bf16[8192,256]{1,0:T(8,128)(2,1)}) %all-gather.2.cloned.1.call-update) | async-done | bytes 4194320 | tf_op jit(solution)/shard_map/all_gather | solution.py:336
  46.0 20.5 %make_tiles.1 = (bf16[8,768,1024]{2,1,0:T(8,128)(2,1)}, bf16[8,768,1024]{2,1,0:T(8,128)(2,1)}, f32[64,128]{1,0:T(8,128)}, f32[64,128]{1,0:T(8,128)}) custom-call(s32[512]{0:T(512)} %and_select_fusion.1.picks, bf16[8192,256]{1,0:T(8,128)(2,1)} %all-gather.2.cloned.1.call-done.frames_ref, bf16[64,128,256]{2,1,0:T(8,128)(2,1)} %bitcast.11), custom_call_target="tpu_custom_call" | custom-call | tf_op jit(solution)/shard_map/make_tiles/pallas_call | solution.py:59
  66.5 1.5 broadcast_in_dim.36
  68.0 4.9 all-to-all-start
  72.9 0.7 bitcast_select_fusion.picks_ref
  73.5 5.4 %all-to-all-done.pieces_ref = f32[8,64,128]{2,1,0:T(8,128)S(1)} async-done(((f32[8,64,128]{2,1,0:T(8,128)}), f32[8,64,128]{2,1,0:T(8,128)S(1)}, u32[]{:S(2)}, u32[]{:S(2)}) %all-to-all-start) | async-done | bytes 262176 | tf_op jit(solution)/shard_map/all_to_all | solution.py:352
  78.9 0.7 copy-done.1
  79.6 11.0 %column_pass.3 = (f32[64,128]{1,0:T(8,128)}, f32[32,64,128]{2,1,0:T(8,128)}) custom-call(s32[512]{0:T(512)} %and_select_fusion.1.picks, f32[8,64,128]{2,1,0:T(8,128)} %copy-done.1, f32[64,128]{1,0:T(8,128)} %get-tuple-element.11.high_ref, s32[8,64]{1,0:T(8,128)} %bitcast_select_fusion.picks_ref, bf16[8,768,1024]{2,1,0:T(8,128)(2,1)} %get-tuple-element.12.exp_ref, ...), custom_call_target="tpu_custom_call" | custom-call | tf_op jit(solution)/shard_map/column_pass/pallas_call | solution.py:256
  90.6 10.1 %all-to-all-start.1 = ((f32[32,64,128]{2,1,0:T(8,128)}), f32[32,64,128]{2,1,0:T(8,128)S(1)}, u32[]{:S(2)}, u32[]{:S(2)}) async-start(f32[32,64,128]{2,1,0:T(8,128)} %get-tuple-element.14), calls=%async_computation.1 | async-start | bytes 2097152 | tf_op jit(solution)/shard_map/all_to_all | solution.py:356
  100.7 0.1 copy.18
  100.8 0.6 and_select_fusion.picks_ref
  101.5 27.4 %all-to-all-done.1.pieces_ref = f32[32,64,128]{2,1,0:T(8,128)S(1)} async-done(((f32[32,64,128]{2,1,0:T(8,128)}), f32[32,64,128]{2,1,0:T(8,128)S(1)}, u32[]{:S(2)}, u32[]{:S(2)}) %all-to-all-start.1) | async-done | bytes 1048608 | tf_op jit(solution)/shard_map/all_to_all | solution.py:356
  128.9 1.1 copy-done
  129.9 10.1 %row_pass.2 = f32[8,64,128]{2,1,0:T(8,128)} custom-call(s32[512]{0:T(512)} %and_select_fusion.1.picks, f32[32,64,128]{2,1,0:T(8,128)} %copy-done, f32[64,128]{1,0:T(8,128)} %get-tuple-element.11.high_ref, s32[64,8]{1,0:T(8,128)} %and_select_fusion.picks_ref, bf16[8,768,1024]{2,1,0:T(8,128)(2,1)} %get-tuple-element.12.exp_ref, ...), custom_call_target="tpu_custom_call" | custom-call | tf_op jit(solution)/shard_map/row_pass/pallas_call | solution.py:294
  140.0 99.8 %all_to_all.30.pieces_ref = f32[8,64,128]{2,1,0:T(8,128)} all-to-all(f32[8,64,128]{2,1,0:T(8,128)} %row_pass.2), channel_id=1, replica_groups=mesh['frames_0'=4,'frames_1'=8,'codes_0'=4,'codes_1'=2] {'codes_0','code..., dimensions={0} | all-to-all | bytes 524288 | tf_op jit(solution)/shard_map/all_to_all | solution.py:352
  239.8 11.0 %column_pass.4 = (f32[64,128]{1,0:T(8,128)}, f32[32,64,128]{2,1,0:T(8,128)}) custom-call(s32[512]{0:T(512)} %and_select_fusion.1.picks, f32[8,64,128]{2,1,0:T(8,128)} %all_to_all.30.pieces_ref, f32[64,128]{1,0:T(8,128)} %get-tuple-element.11.high_ref, s32[8,64]{1,0:T(8,128)} %bitcast_select_fusion.picks_ref, ...), custom_call_target="tpu_custom_call" | custom-call | tf_op jit(solution)/shard_map/column_pass/pallas_call | solution.py:256
  250.8 36.7 %all_to_all.31.pieces_ref = f32[32,64,128]{2,1,0:T(8,128)} all-to-all(f32[32,64,128]{2,1,0:T(8,128)} %get-tuple-element.15), channel_id=1, replica_groups=mesh['frames_0'=4,'frames_1'=8,'codes_0'=4,'codes_1'=2] {'frames_0','fra..., dimensions={0} | all-to-all | bytes 2097152 | tf_op jit(solution)/shard_map/all_to_all | solution.py:356
  287.5 10.1 %row_pass.3 = f32[8,64,128]{2,1,0:T(8,128)} custom-call(s32[512]{0:T(512)} %and_select_fusion.1.picks, f32[32,64,128]{2,1,0:T(8,128)} %all_to_all.31.pieces_ref, f32[64,128]{1,0:T(8,128)} %get-tuple-element.11.high_ref, s32[64,8]{1,0:T(8,128)} %and_select_fusion.picks_ref, bf16[8,768,1024]{2,1,0:T(8,128)(2,1)} %get-tuple-element.12.exp_ref, ...), custom_call_target="tpu_custom_call" | custom-call | tf_op jit(solution)/shard_map/row_pass/pallas_call | solution.py:294
  297.6 100.5 %all_to_all.32.pieces_ref = f32[8,64,128]{2,1,0:T(8,128)} all-to-all(f32[8,64,128]{2,1,0:T(8,128)} %row_pass.3), channel_id=1, replica_groups=mesh['frames_0'=4,'frames_1'=8,'codes_0'=4,'codes_1'=2] {'codes_0','code..., dimensions={0} | all-to-all | bytes 524288 | tf_op jit(solution)/shard_map/all_to_all | solution.py:352
  398.0 11.0 %column_pass.5 = (f32[64,128]{1,0:T(8,128)}, f32[32,64,128]{2,1,0:T(8,128)}) custom-call(s32[512]{0:T(512)} %and_select_fusion.1.picks, f32[8,64,128]{2,1,0:T(8,128)} %all_to_all.32.pieces_ref, f32[64,128]{1,0:T(8,128)} %get-tuple-element.11.high_ref, s32[8,64]{1,0:T(8,128)} %bitcast_select_fusion.picks_ref, ...), custom_call_target="tpu_custom_call" | custom-call | tf_op jit(solution)/shard_map/column_pass/pallas_call | solution.py:256
  409.0 81.6 %all_to_all.33 = f32[32,64,128]{2,1,0:T(8,128)S(1)} all-to-all(f32[32,64,128]{2,1,0:T(8,128)} %get-tuple-element.17), channel_id=1, replica_groups=mesh['frames_0'=4,'frames_1'=8,'codes_0'=4,'codes_1'=2] {'frames_0','fra..., dimensions={0} | all-to-all | bytes 2097152 | tf_op jit(solution)/shard_map/all_to_all | solution.py:356
  490.6 0.1 reduce_max.25
  490.7 0.2 exponential_reduce_fusion
  490.9 0.6 subtract_bitcast_fusion
  (6 shorter events, 0.0 us)
Async XLA Ops:
  7.2 38.9 %all-gather.2.cloned.1.call-start = ((), (), s32[]{:S(2)}) async-start(), calls=%async_computation.6 | async-start | bytes 4718592 | tf_op jit(solution)/shard_map/all_gather | solution.py:336
  68.0 11.0 %all-to-all-start = ((f32[8,64,128]{2,1,0:T(8,128)}), f32[8,64,128]{2,1,0:T(8,128)S(1)}, u32[]{:S(2)}, u32[]{:S(2)}) async-start(f32[8,64,128]{2,1,0:T(8,128)} %broadcast_in_dim.36), calls=%async_computation | async-start | bytes 524288 | tf_op jit(solution)/shard_map/all_to_all | solution.py:352
  78.9 0.7 copy-start.1
  90.6 38.2 %all-to-all-start.1 = ((f32[32,64,128]{2,1,0:T(8,128)}), f32[32,64,128]{2,1,0:T(8,128)S(1)}, u32[]{:S(2)}, u32[]{:S(2)}) async-start(f32[32,64,128]{2,1,0:T(8,128)} %get-tuple-element.14), calls=%async_computation.1 | async-start | bytes 2097152 | tf_op jit(solution)/shard_map/all_to_all | solution.py:356
  128.9 1.1 copy-start
Sparse Core Ops, SparseCore 0:
  9.8 36.1 all-gather.1

commit v2 on v1

--- a/solution.py
+++ b/solution.py
@@ -21,7 +21,7 @@
 NEG_FILL = -1e30
 NEG_ROW = -1e29
 SMALL = 1e-26
-VMEM = 56 * 1024 * 1024
+VMEM = 14 * 1024 * 1024
 
 
 def tiles_kernel(picks, frames_ref, codes_ref, exp_ref, logit_ref, high_ref, lse_ref):
@@ -338,7 +338,9 @@
     num_blocks = codes.shape[0] // BLK
     frame_count = pattern.shape[0]
     picked = candidates(pattern, lax.axis_index(CODES) * num_blocks)
-    picks = picked.reshape(-1)
+    picks, picked, picked_t, gathered = lax.optimization_barrier(
+        (picked.reshape(-1), picked, picked.T, gathered)
+    )
     frames_total = frame_count * BLK * lax.axis_size(FRAMES)
     codes_total = num_blocks * BLK * lax.axis_size(CODES)
     log_ratio = math.log(frames_total / codes_total)
@@ -351,7 +353,7 @@
     for iteration in range(ITERS):
         pieces = lax.all_to_all(pieces, CODES, 0, 0, tiled=True)
         row_potential, pieces = column_pass(
-            picks, pieces, high, picked.T, exps, logits, frame_copies
+            picks, pieces, high, picked_t, exps, logits, frame_copies
         )
         pieces = lax.all_to_all(pieces, FRAMES, 0, 0, tiled=True)
         if iteration < ITERS - 1:

time: 507 us -> 419 us (0.83)
  the two profiles are of different devices: /device:TPU:34 before, /device:TPU:7 now
where the time goes in v2:
time: 419 us; the launch traced here: 418 us
  Pallas kernels  242 us (58%)
  blocking collectives  118 us (28%)
  waiting for transfers between devices  37.3 us (9%)
  between operations  14.1 us (3%)
  local copies, waits for them, and re-layouts  4.78 us (1%)
    pallas_call x3, Pallas kernels, column_pass(): pl.pallas_call(functools.partial(column_kernel, copies), grid_spec=pltpu....  140 us
    all_to_all x3, blocking collectives, shards(): pieces = lax.all_to_all(pieces, FRAMES, 0, 0, tiled=True)  90.4 us
    pallas_call x2, Pallas kernels, row_pass(): pl.pallas_call(functools.partial(row_kernel, copies, log_ratio), grid_spe...  87.4 us
    all_gather x1, waiting for transfers between devices, shards(): gathered = lax.all_gather(frames, CODES, axis=0, tiled=True)  36.7 us
    all_to_all x3, blocking collectives, shards(): pieces = lax.all_to_all(pieces, CODES, 0, 0, tiled=True)  27.5 us
    pallas_call x1, Pallas kernels, make_tiles(): pl.pallas_call(tiles_kernel, grid_spec=pltpu.PrefetchScalarGridSpec(num_s...  15.1 us
  transfers between devices with their start and end apart: 1, of which 1 were waited for; matrix products, arithmetic and copies ran while one was open for 0% of the time, Pallas kernels for 0%

profile of v2, /device:TPU:7, one launch (start us, length us, event | category | flops | bytes accessed | tf_op | source)
XLA Modules:
  0.0 418.0 jit_solution(14725348121414894826)
XLA Ops:
  7.2 0.0 all-gather.2.cloned.1.call-start
  7.2 0.7 all-gather.2.cloned.1.call-update
  7.9 0.1 and.23
  8.0 0.8 convert_reduce_fusion
  8.8 0.1 select_reduce_fusion
  8.9 0.1 copy.17
  8.9 0.1 copy.18
  9.1 0.1 reduce_max.23
  9.2 0.1 bitcast_select_fusion.picks_ref
  9.2 36.7 %all-gather.2.cloned.1.call-done.frames_ref = bf16[8192,256]{1,0:T(8,128)(2,1)} async-done(((bf16[1024,256]{1,0:T(8,128)(2,1)}), bf16[8192,256]{1,0:T(8,128)(2,1)}) %all-gather.2.cloned.1.call-update) | async-done | bytes 4194320 | tf_op jit(solution)/shard_map/all_gather | solution.py:336
  45.9 0.0 copy-start
  45.9 2.2 copy-done
  48.1 0.0 copy-start.1
  48.1 2.2 copy-done.1
  50.3 15.1 %make_tiles.1 = (bf16[8,768,1024]{2,1,0:T(8,128)(2,1)S(1)}, bf16[8,768,1024]{2,1,0:T(8,128)(2,1)S(1)}, f32[64,128]{1,0:T(8,128)S(1)}, f32[64,128]{1,0:T(8,128)S(1)}) custom-call(s32[512]{0:T(512)S(1)} %and_select_fusion.1.picks, bf16[8192,256]{1,0:T(8,128)(2,1)S(1)} %copy-done.1, bf16[64,128,256]{2,1,0:T(8,128)(2,1)S(1)} %bitcast.11), custom_call_target="tpu_custom_call" | custom-call | tf_op jit(solution)/shard_map/make_tiles/pallas_call | solution.py:59
  65.4 9.8 %all_to_all.30.pieces_ref = f32[8,64,128]{2,1,0:T(8,128)S(1)} all-to-all(f32[8,64,128]{2,1,0:T(8,128)S(1)} %broadcast_in_dim.38), channel_id=1, replica_groups=mesh['frames_0'=4,'frames_1'=8,'codes_0'=4,'codes_1'=2] {'codes_0','code..., dimensions={0} | all-to-all | bytes 524288 | tf_op jit(solution)/shard_map/all_to_all | solution.py:354
  75.2 46.5 %column_pass.3 = (f32[64,128]{1,0:T(8,128)}, f32[32,64,128]{2,1,0:T(8,128)S(1)}) custom-call(s32[512]{0:T(512)S(1)} %and_select_fusion.1.picks, f32[8,64,128]{2,1,0:T(8,128)S(1)} %all_to_all.30.pieces_ref, f32[64,128]{1,0:T(8,128)S(1)} %get-tuple-element.17.high_ref, s32[8,64]{1,0:T(8,128)S(1)} %bitcast_select_fusion.picks_ref, ...), custom_call_target="tpu_custom_call" | custom-call | tf_op jit(solution)/shard_map/column_pass/pallas_call | solution.py:256
  121.8 28.8 %all_to_all.31.pieces_ref = f32[32,64,128]{2,1,0:T(8,128)S(1)} all-to-all(f32[32,64,128]{2,1,0:T(8,128)S(1)} %get-tuple-element.21), channel_id=1, replica_groups=mesh['frames_0'=4,'frames_1'=8,'codes_0'=4,'codes_1'=2] {'frames_0','fra..., dimensions={0} | all-to-all | bytes 2097152 | tf_op jit(solution)/shard_map/all_to_all | solution.py:358
  150.6 43.7 %row_pass.2 = f32[8,64,128]{2,1,0:T(8,128)S(1)} custom-call(s32[512]{0:T(512)S(1)} %and_select_fusion.1.picks, f32[32,64,128]{2,1,0:T(8,128)S(1)} %all_to_all.31.pieces_ref, f32[64,128]{1,0:T(8,128)S(1)} %get-tuple-element.17.high_ref, s32[64,8]{1,0:T(8,128)S(1)} %and_select_fusion.picks_ref, bf16[8,768,1024]{2,1,0:T(8,128)(2,1)S(1)} %get-tuple-element.19.exp_ref, ...), custom_call_target="tpu_custom_call" | custom-call | tf_op jit(solution)/shard_map/row_pass/pallas_call | solution.py:294
  194.3 8.8 %all_to_all.32.pieces_ref = f32[8,64,128]{2,1,0:T(8,128)S(1)} all-to-all(f32[8,64,128]{2,1,0:T(8,128)S(1)} %row_pass.2), channel_id=1, replica_groups=mesh['frames_0'=4,'frames_1'=8,'codes_0'=4,'codes_1'=2] {'codes_0','code..., dimensions={0} | all-to-all | bytes 524288 | tf_op jit(solution)/shard_map/all_to_all | solution.py:354
  203.1 46.5 %column_pass.4 = (f32[64,128]{1,0:T(8,128)}, f32[32,64,128]{2,1,0:T(8,128)S(1)}) custom-call(s32[512]{0:T(512)S(1)} %and_select_fusion.1.picks, f32[8,64,128]{2,1,0:T(8,128)S(1)} %all_to_all.32.pieces_ref, f32[64,128]{1,0:T(8,128)S(1)} %get-tuple-element.17.high_ref, s32[8,64]{1,0:T(8,128)S(1)} %bitcast_select_fusion.picks_ref, ...), custom_call_target="tpu_custom_call" | custom-call | tf_op jit(solution)/shard_map/column_pass/pallas_call | solution.py:256
  249.6 26.9 %all_to_all.33.pieces_ref = f32[32,64,128]{2,1,0:T(8,128)S(1)} all-to-all(f32[32,64,128]{2,1,0:T(8,128)S(1)} %get-tuple-element.23), channel_id=1, replica_groups=mesh['frames_0'=4,'frames_1'=8,'codes_0'=4,'codes_1'=2] {'frames_0','fra..., dimensions={0} | all-to-all | bytes 2097152 | tf_op jit(solution)/shard_map/all_to_all | solution.py:358
  276.5 43.7 %row_pass.3 = f32[8,64,128]{2,1,0:T(8,128)S(1)} custom-call(s32[512]{0:T(512)S(1)} %and_select_fusion.1.picks, f32[32,64,128]{2,1,0:T(8,128)S(1)} %all_to_all.33.pieces_ref, f32[64,128]{1,0:T(8,128)S(1)} %get-tuple-element.17.high_ref, s32[64,8]{1,0:T(8,128)S(1)} %and_select_fusion.picks_ref, bf16[8,768,1024]{2,1,0:T(8,128)(2,1)S(1)} %get-tuple-element.19.exp_ref, ...), custom_call_target="tpu_custom_call" | custom-call | tf_op jit(solution)/shard_map/row_pass/pallas_call | solution.py:294
  320.2 8.8 %all_to_all.34.pieces_ref = f32[8,64,128]{2,1,0:T(8,128)S(1)} all-to-all(f32[8,64,128]{2,1,0:T(8,128)S(1)} %row_pass.3), channel_id=1, replica_groups=mesh['frames_0'=4,'frames_1'=8,'codes_0'=4,'codes_1'=2] {'codes_0','code..., dimensions={0} | all-to-all | bytes 524288 | tf_op jit(solution)/shard_map/all_to_all | solution.py:354
  329.1 46.5 %column_pass.5 = (f32[64,128]{1,0:T(8,128)}, f32[32,64,128]{2,1,0:T(8,128)S(1)}) custom-call(s32[512]{0:T(512)S(1)} %and_select_fusion.1.picks, f32[8,64,128]{2,1,0:T(8,128)S(1)} %all_to_all.34.pieces_ref, f32[64,128]{1,0:T(8,128)S(1)} %get-tuple-element.17.high_ref, s32[8,64]{1,0:T(8,128)S(1)} %bitcast_select_fusion.picks_ref, ...), custom_call_target="tpu_custom_call" | custom-call | tf_op jit(solution)/shard_map/column_pass/pallas_call | solution.py:256
  375.6 34.7 %all_to_all.35 = f32[32,64,128]{2,1,0:T(8,128)S(1)} all-to-all(f32[32,64,128]{2,1,0:T(8,128)S(1)} %get-tuple-element.25), channel_id=1, replica_groups=mesh['frames_0'=4,'frames_1'=8,'codes_0'=4,'codes_1'=2] {'frames_0','fra..., dimensions={0} | all-to-all | bytes 2097152 | tf_op jit(solution)/shard_map/all_to_all | solution.py:358
  410.3 0.1 reduce_max.25
  410.4 0.2 exponential_reduce_fusion
  410.6 0.6 subtract_bitcast_fusion
  (7 shorter events, 0.1 us)
Async XLA Ops:
  7.2 38.7 %all-gather.2.cloned.1.call-start = ((), (), s32[]{:S(2)}) async-start(), calls=%async_computation.6 | async-start | bytes 4718592 | tf_op jit(solution)/shard_map/all_gather | solution.py:336
  45.9 2.2 copy-start
  48.1 2.2 copy-start.1
Sparse Core Ops, SparseCore 0:
  9.8 36.0 all-gather.1
